TPU v7x, 32 devices: a whole 2x2x4 slice. The times are simulated.
32 devices in a mesh: chars: 2 (over x), prow: 16 (over z, y, core).
Axes of the slice: x: 2, y: 2, z: 4, core: 2. Of those that a mesh axis runs over, the one named last changes fastest.
Arguments:
- queries: bfloat16 [8192, 512], P(('chars', 'prow')), parts along dimension 0, may hold values from -8 to 8
- keys: bfloat16 [8192, 512], P(('chars', 'prow')), parts along dimension 0, may hold values from -8 to 8
- values: bfloat16 [8192, 512], P(('chars', 'prow')), parts along dimension 0, may hold values from -6 to 6
- out_grad: bfloat16 [8192, 512], P(('chars', 'prow')), parts along dimension 0, may hold values from -6 to 6
- valid_counts: int32 [32, 4], P('chars'), parts along dimension 0, may hold values from 1 to 64
- landmark_cols: int32 [32], P('chars'), parts along dimension 0, may hold values from 0 to 3
- landmark_rows: int32 [32, 4], P(('chars', 'prow')), parts along dimension 0, may hold values from 0 to 15, as said below
Outputs:
- attn_out: bfloat16 [8192, 512], P(('chars', 'prow')), parts along dimension 0
- query_grad: bfloat16 [8192, 512], P(('chars', 'prow')), parts along dimension 0
- key_grad: bfloat16 [8192, 512], P(('chars', 'prow')), parts along dimension 0
- value_grad: bfloat16 [8192, 512], P(('chars', 'prow')), parts along dimension 0
There are 2 independent parts, one for each index of `chars`. A program takes and returns all parts, laid end to end along the dimension named above; each array names one. Nothing has to cross between parts.
Inputs may be any that keep to these rules, and one draw needn't show every extreme that they name: `landmark_rows`: the 4 entries of each row are distinct.
All inputs are finite; a program needn't handle non-finite values.
Results may differ from a plain program's by a relative error of at most 0.012.
The roundings to bfloat16 on the way count: a program that leaves them out, or rounds other values in their place, can miss the bound.
Values may be sent and summed in bfloat16 or wider, within the bound.
A program may use at most 192 MiB of HBM per device.

v0:
```python
import math

import jax
import jax.numpy as jnp
from jax import lax
from jax.sharding import PartitionSpec as P

HEADS = 8
HD = 64
BLK = 64
NLAND = 4
PC = 4


masked_score = -1e30


def extended(x, sides, width):
    for axis, dim in sides:
        devices, length = (lax.axis_size(axis), x.shape[dim])
        up = [(i, (i + 1) % devices) for i in range(devices - 1)]
        down = [(j, i) for i, j in up]
        last = lax.slice_in_dim(x, length - width, length, axis=dim)
        first = lax.slice_in_dim(x, 0, width, axis=dim)
        before = lax.ppermute(last, axis, up)
        after = lax.ppermute(first, axis, down)
        x = jnp.concatenate([before, x, after], axis=dim)
    return x


def passed_along(block, axis, distance):
    devices = range(lax.axis_size(axis))
    route = [(i - distance, i) for i in devices if i - distance in devices]
    return lax.ppermute(block, axis, route)


def product(form, left, right):
    return jnp.einsum(form, left, right, preferred_element_type=jnp.float32)


def window_stack(near_rows, columns):
    pieces = [
        near_rows[row_off, col_off : col_off + columns]
        for row_off in range(3)
        for col_off in range(3)
    ]
    stacked = jnp.stack(pieces, axis=1)
    return stacked.reshape(columns, 9 * stacked.shape[2], stacked.shape[3])


def window_mask(count_near, columns, block_len):
    pieces = [
        count_near[row_off, col_off : col_off + columns]
        for row_off in range(3)
        for col_off in range(3)
    ]
    counts = jnp.stack(pieces, axis=1)
    position = jnp.arange(block_len)
    return (position[None, None, :] < counts[:, :, None]).reshape(columns, 9 * block_len)


def spread(grad_window, columns, block_len):
    pieces = grad_window.reshape(columns, 9, block_len, grad_window.shape[-1])
    layers = []
    for row_off in range(3):
        left = jnp.pad(pieces[:, row_off * 3], ((0, 2), (0, 0), (0, 0)))
        middle = jnp.pad(pieces[:, row_off * 3 + 1], ((1, 1), (0, 0), (0, 0)))
        right = jnp.pad(pieces[:, row_off * 3 + 2], ((2, 0), (0, 0), (0, 0)))
        layers.append(left + middle + right)
    return jnp.stack(layers)


def attend(
    query_blocks,
    grad_raw,
    keys_win,
    values_win,
    mask_win,
    keys_land,
    values_land,
    mask_land,
    query_valid,
):
    score_scale = 1.0 / math.sqrt(query_blocks.shape[-1])
    scores_win = product("cqhe,cwhe->chqw", query_blocks, keys_win) * score_scale
    scores_land = product("cqhe,lhe->chql", query_blocks, keys_land) * score_scale
    scores_win = jnp.where(mask_win[:, None, None, :], scores_win, masked_score)
    scores_land = jnp.where(mask_land[None, None, None, :], scores_land, masked_score)
    row_max = jnp.maximum(jnp.max(scores_win, axis=-1), jnp.max(scores_land, axis=-1))
    exp_total = jnp.sum(jnp.exp(scores_win - row_max[..., None]), axis=-1) + jnp.sum(
        jnp.exp(scores_land - row_max[..., None]), axis=-1
    )
    log_total = row_max + jnp.log(exp_total)
    probs_win = jnp.exp(scores_win - log_total[..., None])
    probs_land = jnp.exp(scores_land - log_total[..., None])
    low_win = probs_win.astype(jnp.bfloat16)
    low_land = probs_land.astype(jnp.bfloat16)
    mixed_out = product("chqw,cwhe->cqhe", low_win, values_win) + product(
        "chql,lhe->cqhe", low_land, values_land
    )
    query_mask = query_valid[:, :, None, None]
    attn_part = jnp.where(query_mask, mixed_out, 0.0).astype(jnp.bfloat16)
    grad_in = jnp.where(query_mask, grad_raw, jnp.zeros_like(grad_raw))
    row_delta = jnp.sum(grad_in.astype(jnp.float32) * mixed_out, axis=-1)
    row_delta = jnp.transpose(row_delta, (0, 2, 1))[..., None]
    dprob_win = product("cqhe,cwhe->chqw", grad_in, values_win)
    dprob_land = product("cqhe,lhe->chql", grad_in, values_land)
    dscore_win = (probs_win * (dprob_win - row_delta) * score_scale).astype(jnp.bfloat16)
    dscore_land = (probs_land * (dprob_land - row_delta) * score_scale).astype(jnp.bfloat16)
    query_part = (
        product("chqw,cwhe->cqhe", dscore_win, keys_win)
        + product("chql,lhe->cqhe", dscore_land, keys_land)
    ).astype(jnp.bfloat16)
    kgrad_win = product("chqw,cqhe->cwhe", dscore_win, query_blocks)
    vgrad_win = product("chqw,cqhe->cwhe", low_win, grad_in)
    kgrad_land = product("chql,cqhe->lhe", dscore_land, query_blocks)
    vgrad_land = product("chql,cqhe->lhe", low_land, grad_in)
    return (attn_part, query_part, kgrad_win, vgrad_win, kgrad_land, vgrad_land)


def per_device(queries, keys, values, out_grad, valid_counts, landmark_cols, landmark_rows):
    model_width = HEADS * HD
    my_row = lax.axis_index("prow")
    row_total = lax.axis_size("prow")
    position = jnp.arange(BLK)
    key_value = jnp.concatenate([keys, values], axis=1).reshape(1, PC, BLK, 2 * model_width)
    near_rows = extended(key_value, (("prow", 0),), 1)
    near_rows = jnp.pad(near_rows, ((0, 0), (1, 1), (0, 0), (0, 0)))
    count_padded = jnp.pad(valid_counts, ((1, 1), (1, 1)))
    count_near = lax.dynamic_slice_in_dim(count_padded, my_row, 3, 0)
    own_col = lax.dynamic_index_in_dim(landmark_cols, my_row, 0, keepdims=False)
    own_block = lax.dynamic_slice_in_dim(key_value[0], own_col, 1, 0)
    land_panel = lax.all_gather(own_block, "prow", axis=0, tiled=True)
    chosen_rows = landmark_rows[0]
    chosen = jnp.take(land_panel, chosen_rows, axis=0)
    chosen_counts = valid_counts[chosen_rows, landmark_cols[chosen_rows]]
    stacked = window_stack(near_rows, PC)
    keys_win = stacked[..., :model_width].reshape(PC, 9 * BLK, HEADS, HD)
    values_win = stacked[..., model_width:].reshape(PC, 9 * BLK, HEADS, HD)
    mask_win = window_mask(count_near, PC, BLK)
    keys_land = chosen[..., :model_width].reshape(NLAND * BLK, HEADS, HD)
    values_land = chosen[..., model_width:].reshape(NLAND * BLK, HEADS, HD)
    mask_land = (position[None, :] < chosen_counts[:, None]).reshape(NLAND * BLK)
    row_counts = lax.dynamic_index_in_dim(valid_counts, my_row, 0, keepdims=False)
    query_valid = position[None, :] < row_counts[:, None]
    attn_part, query_part, kgrad_win, vgrad_win, kgrad_land, vgrad_land = attend(
        queries.reshape(PC, BLK, HEADS, HD),
        out_grad.reshape(PC, BLK, HEADS, HD),
        keys_win,
        values_win,
        mask_win,
        keys_land,
        values_land,
        mask_land,
        query_valid,
    )
    grad_window = jnp.concatenate(
        [kgrad_win.reshape(PC, 9 * BLK, model_width), vgrad_win.reshape(PC, 9 * BLK, model_width)],
        axis=-1,
    )
    summed = spread(grad_window, PC, BLK)
    own_grads = summed[1, 1 : PC + 1]
    from_above = passed_along(summed[2, 1 : PC + 1], "prow", 1)
    from_below = passed_along(summed[0, 1 : PC + 1], "prow", -1)
    grad_land = jnp.concatenate(
        [kgrad_land.reshape(NLAND, BLK, model_width), vgrad_land.reshape(NLAND, BLK, model_width)],
        axis=-1,
    )
    slot_grads = (
        jnp.zeros((row_total, BLK, 2 * model_width), jnp.float32).at[chosen_rows].add(grad_land)
    )
    land_total = lax.psum_scatter(slot_grads, "prow", scatter_dimension=0, tiled=True)[0]
    hit_mask = (jnp.arange(PC) == own_col)[:, None, None]
    all_grads = own_grads + from_above + from_below + jnp.where(hit_mask, land_total[None], 0.0)
    attn_out = attn_part.reshape(PC * BLK, model_width)
    query_grad = query_part.reshape(PC * BLK, model_width)
    key_grad = all_grads[..., :model_width].astype(jnp.bfloat16).reshape(PC * BLK, model_width)
    value_grad = all_grads[..., model_width:].astype(jnp.bfloat16).reshape(PC * BLK, model_width)
    return (attn_out, query_grad, key_grad, value_grad)


def solution(mesh):
    return jax.shard_map(
        per_device,
        mesh=mesh,
        in_specs=(
            P(("chars", "prow"), None),
            P(("chars", "prow"), None),
            P(("chars", "prow"), None),
            P(("chars", "prow"), None),
            P("chars", None),
            P("chars"),
            P(("chars", "prow"), None),
        ),
        out_specs=(
            P(("chars", "prow"), None),
            P(("chars", "prow"), None),
            P(("chars", "prow"), None),
            P(("chars", "prow"), None),
        ),
        check_vma=False,
    )
```

profile of v0, /device:TPU:1, one launch (start us, length us, event | category | flops | bytes accessed | tf_op | source)
XLA Modules:
  0.0 191.5 jit_solution(16934145135606755180)
XLA Ops:
  7.2 1.0 constant_dynamic-update-slice_fusion.1
  8.2 1.0 constant_dynamic-update-slice_fusion
  9.3 2.0 %collective-permute-start.1 = (bf16[1,4,64,1024]{3,2,1,0:T(8,128)(2,1)S(1)}, bf16[1,4,64,1024]{3,2,1,0:T(8,128)(2,1)S(1)}, u32[]{:S(2)}, u32[]{:S(2)}) collective-permute-start(bf16[1,4,64,1024]{3,2,1,0:T(8,128)(2,1)S(1)} %bitcast.260), channel_id=1, source_target_pairs={{1,0},{2,1},{3,2},{4,3},{5,4},{6,5},{7,6},{8,7},{9,8},{10,9},{11,1... | collective-permute-start | bytes 1572872 | tf_op jit(solution)/shard_map/ppermute | solution.py:26
  11.2 4.5 %collective-permute-start = (bf16[1,4,64,1024]{3,2,1,0:T(8,128)(2,1)S(1)}, bf16[1,4,64,1024]{3,2,1,0:T(8,128)(2,1)S(1)}, u32[]{:S(2)}, u32[]{:S(2)}) collective-permute-start(bf16[1,4,64,1024]{3,2,1,0:T(8,128)(2,1)S(1)} %bitcast.261), channel_id=1, source_target_pairs={{0,1},{1,2},{2,3},{3,4},{4,5},{5,6},{6,7},{7,8},{8,9},{9,10},{10,1... | collective-permute-start | bytes 1572872 | tf_op jit(solution)/shard_map/ppermute | solution.py:25
  15.7 1.2 dynamic_slice.16
  18.9 0.7 constant_dynamic-slice_fusion
  19.7 0.7 fusion.44
  20.3 0.7 compare_and_fusion
  21.0 1.3 gather_fusion
  22.3 0.7 fusion.39
  23.0 0.8 pad_dynamic-slice_fusion
  23.7 1.3 gather_fusion.1
  25.2 0.9 dynamic-slice_reduce_fusion
  26.7 1.0 copy.145
  28.4 1.1 copy.153
  30.4 1.9 %fusion.46 = (bf16[4,576,512]{2,1,0:T(8,128)(2,1)S(1)}, bf16[4,576,512]{2,1,0:T(8,128)(2,1)}) fusion(bf16[4,576,1024]{2,1,0:T(8,128)(2,1)S(1)} %bitcast.259), kind=kLoop, calls=%fused_computation.124 | loop fusion | bytes 9437184 | tf_op jit(solution)/shard_map/slice | solution.py:139
  32.3 2.6 %copy.132 = bf16[4,576,512]{1,2,0:T(8,128)(2,1)} copy(bf16[4,576,512]{2,1,0:T(8,128)(2,1)S(1)} %get-tuple-element.15) | data formatting | bytes 4718592 | tf_op jit(solution)/shard_map/slice | solution.py:139
  34.8 3.1 %copy.142 = bf16[4,576,512]{1,2,0:T(8,128)(2,1)S(1)} copy(bf16[4,576,512]{2,1,0:T(8,128)(2,1)} %get-tuple-element.16) | data formatting | bytes 4718592 | tf_op jit(solution)/shard_map/slice | solution.py:138
  38.0 3.3 %bitcast_reduce_fusion = (f32[4,8,64]{2,1,0:T(8,128)S(1)}, f32[4,8,576,64]{2,3,1,0:T(8,128)}) fusion(pred[4,576]{1,0:T(4,128)(4,1)S(1)} %broadcast_compare_fusion, bf16[4,64,8,64]{1,3,2,0:T(8,128)(2,1)S(1)} %copy.161, bf16[4,576,8,64]{1,3,2,0:T(8,128)(2,1)S(1)} %bitcast.256), kind=kOutput, calls=%fused_computation.8 | convolution fusion | flops 154531840 | bytes 7350528 | tf_op jit(solution)/shard_map/cqhe,cwhe->chqw/dot_general | solution.py:38
  41.3 20.8 %all-gather.2.cloned.1.call-done = bf16[16,64,1024]{2,1,0:T(8,128)(2,1)} async-done(((bf16[1,64,1024]{2,1,0:T(8,128)(2,1)}), bf16[16,64,1024]{2,1,0:T(8,128)(2,1)}) %all-gather.2.cloned.1.call-update) | async-done | bytes 2097168 | tf_op jit(solution)/shard_map/all_gather | solution.py:133
  62.1 2.2 %gather_fusion.2 = bf16[4,64,1024]{2,1,0:T(8,128)(2,1)S(1)} fusion(bf16[16,64,1024]{2,1,0:T(8,128)(2,1)} %all-gather.2.cloned.1.call-done, s32[1024]{0:T(1024)S(1)} %pad_clamp_fusion), kind=kCustom, calls=%fused_computation.2 | custom fusion | bytes 1048592 | tf_op jit(solution)/shard_map/jit(_take)/gather | solution.py:135
  64.7 1.0 copy.150
  67.2 0.9 fusion.11
  68.1 0.8 copy-done
  68.9 1.4 fusion.1
  70.3 0.7 convolution_bitcast_fusion.4
  71.0 1.0 copy-done.10
  72.0 2.4 %select_convert_fusion = (bf16[4,64,8,64]{1,3,2,0:T(8,128)(2,1)}, f32[4,64,8,64]{1,3,2,0:T(8,128)S(1)}) fusion(pred[4,64]{1,0:T(4,128)(4,1)S(1)} %iota_compare_fusion.3, f32[4,64,8,64]{1,3,2,0:T(8,128)S(1)} %convolution_bitcast_fusion.4, bf16[4,576,8,64]{1,3,2,0:T(8,128)(2,1)S(1)} %bitcast.266, f32[4,8,576,64]{2,3,1,0:T(8,128)S(1)} %copy-done, ...), kind=kOutput, calls=%fused_computation.63 | convolution fusion | flops 155975680 | bytes 8399360 | tf_op jit(solution)/shard_map/chqw,cwhe->cqhe/dot_general | solution.py:38
  74.6 1.1 copy.156
  75.7 1.5 convolution_bitcast_fusion.7
  77.2 2.5 %reshape.234 = f32[4,64,512]{1,0,2:T(4,128)} reshape(f32[256,8,64]{0,2,1:T(8,128)} %convolution_bitcast_fusion.7) | data formatting | bytes 1048576 | tf_op jit(solution)/shard_map/reshape | solution.py:166
  79.7 2.4 %copy.179 = f32[4,64,512]{2,1,0:T(8,128)} copy(f32[4,64,512]{1,0,2:T(4,128)} %reshape.234) | data formatting | bytes 1048576 | tf_op jit(solution)/shard_map/reshape | solution.py:166
  82.1 1.5 fusion.50
  83.6 0.8 multiply_convert_fusion.1
  84.4 1.0 copy-done.5
  86.7 2.5 %broadcast_in_dim.107 = f32[16,64,1024]{2,1,0:T(8,128)} broadcast(f32[]{:T(128)} %constant.32.clone.1), dimensions={} | broadcast | bytes 4194308 | tf_op jit(solution)/shard_map/broadcast_in_dim | solution.py:170
  89.2 3.1 %scatter_fusion = f32[16,64,1024]{2,1,0:T(8,128)} fusion(f32[16,64,1024]{2,1,0:T(8,128)} %broadcast_in_dim.107, s32[4]{0:T(128)S(1)} %fusion.44, f32[4,64,1024]{2,1,0:T(8,128)S(1)} %pad_maximum_fusion), kind=kCustom, calls=%fused_computation.3 | custom fusion | flops 262144 | bytes 3145744 | tf_op jit(solution)/shard_map/scatter-add | solution.py:170
  92.4 1.0 copy-done.9
  93.4 5.3 %multiply_convert_fusion = bf16[4,8,64,576]{3,2,1,0:T(8,128)(2,1)S(1)} fusion(f32[4,8,576,64]{2,3,1,0:T(8,128)} %get-tuple-element.31, f32[4,8,64]{2,1,0:T(8,128)S(1)} %bitcast.273, f32[4,8,64]{2,1,0:T(8,128)S(1)} %fusion.35, pred[4,576]{1,0:T(4,128)(4,1)S(1)} %broadcast_compare_fusion, bf16[4,64,8,64]{1,3,2,0:T(8,128)(2,1)S(1)} %copy-done.9, ...), kind=kOutput, calls=%fused_computation.12 | convolution fusion | flops 159252480 | bytes 9718016 | tf_op jit(solution)/shard_map/cqhe,cwhe->chqw/dot_general | solution.py:38
  98.7 1.5 copy-done.4
  100.2 3.1 %convolution_bitcast_fusion = f32[4,576,8,64]{1,3,2,0:T(8,128)} fusion(bf16[4,64,8,64]{1,3,2,0:T(8,128)(2,1)S(1)} %copy.161, bf16[4,8,64,576]{3,2,1,0:T(8,128)(2,1)S(1)} %multiply_convert_fusion), kind=kOutput, calls=%fused_computation.19 | convolution fusion | flops 150994944 | bytes 7340032 | tf_op jit(solution)/shard_map/chqw,cqhe->cwhe/dot_general | solution.py:38
  103.2 8.5 %copy.162 = f32[4,576,8,64]{3,2,1,0:T(8,128)} copy(f32[4,576,8,64]{1,3,2,0:T(8,128)} %convolution_bitcast_fusion) | data formatting | bytes 9437184 | tf_op jit(solution)/shard_map/chqw,cqhe->cwhe/transpose | solution.py:38
  111.7 9.0 %concatenate.23 = f32[4,9,64,512]{3,2,1,0:T(8,128)} reshape(f32[4,576,8,64]{3,2,1,0:T(8,128)} %copy.162) | data formatting | bytes 9437184 | tf_op jit(solution)/shard_map/concatenate | solution.py:157
  120.7 6.1 %convolution_bitcast_fusion.1 = f32[4,576,8,64]{1,3,2,0:T(8,128)} fusion(bf16[4,64,8,64]{1,3,2,0:T(8,128)(2,1)S(1)} %copy-done.9, f32[4,8,576,64]{2,3,1,0:T(8,128)} %get-tuple-element.31, f32[4,8,64]{2,1,0:T(8,128)S(1)} %fusion.35, pred[4,576]{1,0:T(4,128)(4,1)S(1)} %broadcast_compare_fusion), kind=kOutput, calls=%fused_computation.20 | convolution fusion | flops 155713536 | bytes 9709824 | tf_op jit(solution)/shard_map/chqw,cqhe->cwhe/dot_general | solution.py:38
  126.8 8.2 %copy.163 = f32[4,576,8,64]{3,2,1,0:T(8,128)} copy(f32[4,576,8,64]{1,3,2,0:T(8,128)} %convolution_bitcast_fusion.1) | data formatting | bytes 9437184 | tf_op jit(solution)/shard_map/chqw,cqhe->cwhe/transpose | solution.py:38
  135.0 9.0 %concatenate.24 = f32[4,9,64,512]{3,2,1,0:T(8,128)} reshape(f32[4,576,8,64]{3,2,1,0:T(8,128)} %copy.163) | data formatting | bytes 9437184 | tf_op jit(solution)/shard_map/concatenate | solution.py:157
  144.0 3.0 %constant_dynamic-update-slice_fusion.4 = f32[4,9,64,1024]{3,2,1,0:T(8,128)S(1)} fusion(f32[4,9,64,512]{3,2,1,0:T(8,128)} %concatenate.23), kind=kLoop, calls=%fused_computation.88 | loop fusion | bytes 9437184
  147.1 0.7 copy-done.3
  147.8 0.5 constant_dynamic-update-slice_fusion.3
  148.3 2.8 %slice_bitcast_fusion.11 = (f32[4,64,1024]{2,1,0:T(8,128)}, f32[4,64,1024]{2,1,0:T(8,128)S(1)}, f32[4,64,1024]{2,1,0:T(8,128)S(1)}, f32[4,64,1024]{2,1,0:T(8,128...) fusion(f32[4,9,64,1024]{3,2,1,0:T(8,128)S(1)} %constant_dynamic, ...), kind=kLoop, calls=%fused_computation.59 | loop fusion | bytes 18874368 | tf_op jit(solution)/shard_map/squeeze | solution.py:66
  151.4 1.1 slice_bitcast_fusion
  152.4 2.2 %collective-permute-start.3 = (f32[4,64,1024]{2,1,0:T(8,128)}, f32[4,64,1024]{2,1,0:T(8,128)}, u32[]{:S(2)}, u32[]{:S(2)}) collective-permute-start(f32[4,64,1024]{2,1,0:T(8,128)} %slice_bitcast_fusion), channel_id=1, source_target_pairs={{1,0},{2,1},{3,2},{4,3},{5,4},{6,5},{7,6},{8,7},{9,8},{10,9},{11,1... | collective-permute-start | bytes 3145736 | tf_op jit(solution)/shard_map/ppermute | solution.py:34
  154.9 1.1 slice_bitcast_fusion.4
  156.0 3.8 %collective-permute-start.2 = (f32[4,64,1024]{2,1,0:T(8,128)}, f32[4,64,1024]{2,1,0:T(8,128)}, u32[]{:S(2)}, u32[]{:S(2)}) collective-permute-start(f32[4,64,1024]{2,1,0:T(8,128)} %slice_bitcast_fusion.4), channel_id=1, source_target_pairs={{0,1},{1,2},{2,3},{3,4},{4,5},{5,6},{6,7},{7,8},{8,9},{9,10},{10,1... | collective-permute-start | bytes 3145736 | tf_op jit(solution)/shard_map/ppermute | solution.py:34
  159.8 0.7 iota_compare_fusion.4
  160.5 1.4 copy.152
  161.8 1.0 reshape.188
  162.9 1.8 convolution_bitcast_fusion.2
  164.7 2.7 %fusion.16 = bf16[4,64,8,64]{1,3,2,0:T(8,128)(2,1)S(1)} fusion(f32[4,64,8,64]{1,3,2,0:T(8,128)S(1)} %convolution_bitcast_fusion.2, bf16[4,576,8,64]{1,3,2,0:T(8,128)(2,1)S(1)} %bitcast.257, bf16[4,8,64,576]{3,2,1,0:T(8,128)(2,1)} %copy-done.4), kind=kOutput, calls=%fused_computation.41 | convolution fusion | flops 151257088 | bytes 5505024 | tf_op jit(solution)/shard_map/chqw,cwhe->cqhe/dot_general | solution.py:38
  167.8 1.0 reshape.190
  168.8 2.1 %add_bitcast_fusion.2 = f32[1,6,64,1024]{3,2,1,0:T(8,128)S(1)} fusion(f32[4,64,1024]{2,1,0:T(8,128)} %get-tuple-element.11, f32[4,64,1024]{2,1,0:T(8,128)} %get-tuple-element.12, f32[4,64,1024]{2,1,0:T(8,128)} %get-tuple-element.6), kind=kLoop, calls=%fused_computation.34 | loop fusion | flops 786432 | bytes 4718592 | tf_op jit(solution)/shard_map/stack | solution.py:70
  170.9 10.9 %collective-permute-done.2 = f32[4,64,1024]{2,1,0:T(8,128)} collective-permute-done((f32[4,64,1024]{2,1,0:T(8,128)}, f32[4,64,1024]{2,1,0:T(8,128)}, u32[]{:S(2)}, u32[]{:S(2)}) %collective-permute-start.2) | collective-permute-done | bytes 1048608 | tf_op jit(solution)/shard_map/ppermute | solution.py:34
  181.9 2.0 %fusion.20 = bf16[4,64,1024]{2,1,0:T(8,128)(2,1)S(1)} fusion(f32[4,64,1024]{2,1,0:T(8,128)} %collective-permute-done.3, f32[4,64,1024]{2,1,0:T(8,128)} %collective-permute-done.2, f32[1,6,64,1024]{3,2,1,0:T(8,128)S(1)} %add_bitcast_fusion.2, f32[64,1024]{1,0:T(8,128)} %bitcast.269, pred[4]{0:T(512)(128)(4,1)S(1)} %iota_compare_fusion.4), kind=kLoop, calls=%fused_computation.56 | loop fusion | flops 1310720 | bytes 3932164 | tf_op jit(solution)/shard_map/convert.1
  183.9 0.8 fusion.47
  (80 shorter events, 6.5 us)
Async XLA Ops:
  7.2 18.9 %copy-start.15 = (bf16[256,512]{1,0:T(8,128)(2,1)S(1)}, bf16[256,512]{1,0:T(8,128)(2,1)}, u32[]{:S(2)}) copy-start(bf16[256,512]{1,0:T(8,128)(2,1)} %param.7) | copy-start | bytes 786436
  7.2 54.9 %all-gather.2.cloned.1.call-start = ((), (), s32[]{:S(2)}) async-start(), calls=%async_computation.1 | async-start | bytes 2228224 | tf_op jit(solution)/shard_map/all_gather | solution.py:133
  8.2 19.9 %copy-start.16 = (bf16[256,512]{1,0:T(8,128)(2,1)S(1)}, bf16[256,512]{1,0:T(8,128)(2,1)}, u32[]{:S(2)}) copy-start(bf16[256,512]{1,0:T(8,128)(2,1)} %param.10) | copy-start | bytes 786436
  9.3 20.4 %collective-permute-start.1 = (bf16[1,4,64,1024]{3,2,1,0:T(8,128)(2,1)S(1)}, bf16[1,4,64,1024]{3,2,1,0:T(8,128)(2,1)S(1)}, u32[]{:S(2)}, u32[]{:S(2)}) collective-permute-start(bf16[1,4,64,1024]{3,2,1,0:T(8,128)(2,1)S(1)} %bitcast.260), channel_id=1, source_target_pairs={{1,0},{2,1},{3,2},{4,3},{5,4},{6,5},{7,6},{8,7},{9,8},{10,9},{11,1... | collective-permute-start | bytes 1572872 | tf_op jit(solution)/shard_map/ppermute | solution.py:26
  11.2 18.4 %collective-permute-start = (bf16[1,4,64,1024]{3,2,1,0:T(8,128)(2,1)S(1)}, bf16[1,4,64,1024]{3,2,1,0:T(8,128)(2,1)S(1)}, u32[]{:S(2)}, u32[]{:S(2)}) collective-permute-start(bf16[1,4,64,1024]{3,2,1,0:T(8,128)(2,1)S(1)} %bitcast.261), channel_id=1, source_target_pairs={{0,1},{1,2},{2,3},{3,4},{4,5},{5,6},{6,7},{7,8},{8,9},{9,10},{10,1... | collective-permute-start | bytes 1572872 | tf_op jit(solution)/shard_map/ppermute | solution.py:25
  19.6 162.3 %reduce-scatter.2.cloned.1.call-start = ((), (), s32[]{:S(2)}) async-start(), calls=%async_computation.2 | async-start | bytes 4456448 | tf_op jit(solution)/shard_map/reduce_scatter | solution.py:172
  26.4 3.6 %copy-start.6 = (bf16[4,64,8,64]{3,2,1,0:T(8,128)(2,1)}, bf16[4,64,8,64]{3,2,1,0:T(8,128)(2,1)S(1)}, u32[]{:S(2)}) copy-start(bf16[4,64,8,64]{3,2,1,0:T(8,128)(2,1)S(1)} %reshape.185) | copy-start | bytes 786436
  37.9 3.3 %copy-start.1 = (bf16[4,576,512]{1,2,0:T(8,128)(2,1)}, bf16[4,576,512]{1,2,0:T(8,128)(2,1)S(1)}, u32[]{:S(2)}) copy-start(bf16[4,576,512]{1,2,0:T(8,128)(2,1)S(1)} %copy.142) | copy-start | bytes 7077892
  64.3 2.1 %copy-start.13 = (bf16[4,64,8,64]{3,1,0,2:T(8,128)(2,1)S(1)}, bf16[4,64,8,64]{3,1,0,2:T(8,128)(2,1)}, u32[]{:S(2)}) copy-start(bf16[4,64,8,64]{3,1,0,2:T(8,128)(2,1)} %copy.145) | copy-start | bytes 786436
  66.4 2.5 %copy-start = (f32[4,8,576,64]{2,3,1,0:T(8,128)S(1)}, f32[4,8,576,64]{2,3,1,0:T(8,128)}, u32[]{:S(2)}) copy-start(f32[4,8,576,64]{2,3,1,0:T(8,128)} %get-tuple-element.31) | copy-start | bytes 14155780
  68.9 1.4 copy-start.14
  70.2 1.7 copy-start.10
  72.0 2.4 %copy-start.11 = (bf16[4,64,8,64]{1,3,2,0:T(8,128)(2,1)S(1)}, bf16[4,64,8,64]{1,3,2,0:T(8,128)(2,1)}, u32[]{:S(2)}) copy-start(bf16[4,64,8,64]{1,3,2,0:T(8,128)(2,1)} %copy.153) | copy-start | bytes 786436
  74.6 5.1 %copy-start.8 = (bf16[4,64,8,64]{1,3,2,0:T(8,128)(2,1)}, bf16[4,64,8,64]{1,3,2,0:T(8,128)(2,1)S(1)}, u32[]{:S(2)}) copy-start(bf16[4,64,8,64]{1,3,2,0:T(8,128)(2,1)S(1)} %get-tuple-element.5) | copy-start | bytes 786436
  83.6 1.8 copy-start.7
  84.4 1.0 copy-start.5
  85.4 1.1 copy-start.12
  92.3 1.0 copy-start.9
  98.7 1.5 copy-start.4
  144.0 3.8 %copy-start.3 = (f32[4,9,64,512]{3,2,1,0:T(8,128)S(1)}, f32[4,9,64,512]{3,2,1,0:T(8,128)}, u32[]{:S(2)}) copy-start(f32[4,9,64,512]{3,2,1,0:T(8,128)} %concatenate.24) | copy-start | bytes 14155780
  152.4 18.5 %collective-permute-start.3 = (f32[4,64,1024]{2,1,0:T(8,128)}, f32[4,64,1024]{2,1,0:T(8,128)}, u32[]{:S(2)}, u32[]{:S(2)}) collective-permute-start(f32[4,64,1024]{2,1,0:T(8,128)} %slice_bitcast_fusion), channel_id=1, source_target_pairs={{1,0},{2,1},{3,2},{4,3},{5,4},{6,5},{7,6},{8,7},{9,8},{10,9},{11,1... | collective-permute-start | bytes 3145736 | tf_op jit(solution)/shard_map/ppermute | solution.py:34
  156.0 8.7 %copy-start.2 = (bf16[4,576,512]{1,2,0:T(8,128)(2,1)S(1)}, bf16[4,576,512]{1,2,0:T(8,128)(2,1)}, u32[]{:S(2)}) copy-start(bf16[4,576,512]{1,2,0:T(8,128)(2,1)} %copy-done.1) | copy-start | bytes 7077892
  156.0 25.9 %collective-permute-start.2 = (f32[4,64,1024]{2,1,0:T(8,128)}, f32[4,64,1024]{2,1,0:T(8,128)}, u32[]{:S(2)}, u32[]{:S(2)}) collective-permute-start(f32[4,64,1024]{2,1,0:T(8,128)} %slice_bitcast_fusion.4), channel_id=1, source_target_pairs={{0,1},{1,2},{2,3},{3,4},{4,5},{5,6},{6,7},{7,8},{8,9},{9,10},{10,1... | collective-permute-start | bytes 3145736 | tf_op jit(solution)/shard_map/ppermute | solution.py:34
Sparse Core Ops, SparseCore 0:
  19.7 42.2 all-gather.1
  92.5 70.2 reduce-scatter.1
where the time goes:
time: 193 us; the launch traced here: 192 us
  local copies, waits for them, and re-layouts  86.8 us (45%)
  waiting for transfers between devices  31.8 us (16%)
  matrix products  29.2 us (15%)
  between operations  16.5 us (9%)
  other arithmetic  14.7 us (8%)
  starting transfers between devices  12.6 us (7%)
    dot_general x10, matrix products, product(): return jnp.einsum(form, left, right, preferred_element_type=jnp.float32)  27.3 us
    all_gather x1, waiting for transfers between devices, per_device(): land_panel = lax.all_gather(own_block, 'prow', axis=0, tiled=True)  20.8 us
    concatenate x3, local copies, waits for them, and re-layouts, per_device(): jnp.concatenate([kgrad_win.reshape(PC, 9 * BLK, model_width), vgrad_win.r...  18.5 us
    transpose x2, local copies, waits for them, and re-layouts, product(): return jnp.einsum(form, left, right, preferred_element_type=jnp.float32)  16.7 us
    ppermute x2, waiting for transfers between devices, passed_along(): return lax.ppermute(block, axis, route)  10.9 us
    unnamed x44, local copies, waits for them, and re-layouts  10.4 us
    ppermute x2, starting transfers between devices, passed_along(): return lax.ppermute(block, axis, route)  6.02 us
    reshape x2, local copies, waits for them, and re-layouts, per_device(): vgrad_land.reshape(NLAND, BLK, model_width)  4.89 us
  transfers between devices with their start and end apart: 6, of which 2 were waited for; matrix products, arithmetic and copies ran while one was open for 48% of the time, Pallas kernels for 0%

commit v1 on v0

v1 whole, which is shorter than its diff:
```python
import functools

import jax
import jax.numpy as jnp
from jax import lax
from jax.experimental import pallas as pl
from jax.experimental.pallas import tpu as pltpu
from jax.sharding import PartitionSpec as P

HEADS = 8
HD = 64
BLK = 64
NLAND = 4
PC = 4
WIDTH = HEADS * HD
ROWS = PC * BLK
KEYS = 3 * ROWS + NLAND * BLK
F32 = jnp.float32
BF16 = jnp.bfloat16
MESH = pl.DeviceIdType.MESH
masked_score = -1e30
VMEM_LIMIT = 60 * 1024 * 1024


def dot(a, b):
    return lax.dot_general(a, b, (((1,), (0,)), ((), ())), preferred_element_type=F32)


def remote(src, dst, send, recv, device):
    return pltpu.make_async_remote_copy(
        src_ref=src,
        dst_ref=dst,
        send_sem=send,
        recv_sem=recv,
        device_id={"prow": device},
        device_id_type=MESH,
    )


def position(n):
    me = lax.axis_index("prow")
    z, y, c = me // 4, (me // 2) % 2, me % 2
    core = me + 1 - 2 * c
    side = me + 2 - 4 * y
    return me, z, y, c, core, side


def greet(n):
    me, z, y, c, core, side = position(n)
    last = n // 4 - 1
    other = me + 2 * c - 1
    has_other = jnp.logical_and(other >= 0, other < n)
    barrier = pltpu.get_barrier_semaphore()

    def signal(device):
        pl.semaphore_signal(barrier, inc=1, device_id={"prow": device}, device_id_type=MESH)

    signal(core)
    signal(side)
    pl.when(z > 0)(lambda: signal(me - 4))
    pl.when(z < last)(lambda: signal(me + 4))
    pl.when(has_other)(lambda: signal(other))
    count = (
        2
        + jnp.where(z > 0, 1, 0)
        + jnp.where(z < last, 1, 0)
        + jnp.where(has_other, 1, 0)
    )
    pl.semaphore_wait(barrier, count)


def gather_kernel(
    n,
    cols_ref,
    k_ref,
    v_ref,
    ka,
    va,
    kb,
    vb,
    panel,
    recv,
    up_s,
    dn_s,
    core_s,
    side_s,
    win_s,
    win_r,
):
    me, z, y, c, core, side = position(n)
    depth = n // 4
    last = depth - 1
    half = n // 2
    own_col = cols_ref[me]
    panel[me, :, :WIDTH] = k_ref[own_col]
    panel[me, :, WIDTH:] = v_ref[own_col]

    @pl.when(me == 0)
    def _():
        ka[...] = jnp.zeros_like(ka)
        va[...] = jnp.zeros_like(va)

    @pl.when(me == n - 1)
    def _():
        kb[...] = jnp.zeros_like(kb)
        vb[...] = jnp.zeros_like(vb)

    greet(n)

    def hop(slot, sems, device):
        return remote(panel.at[slot], panel.at[slot], sems.at[slot // 2], recv.at[slot], device)

    to_side = remote(panel.at[me], panel.at[me], side_s.at[0], recv.at[me], side)
    to_side.start()

    def up(slot):
        return hop(slot, up_s, me + 4)

    def down(slot):
        return hop(slot, dn_s, me - 4)

    def over(slot):
        return hop(slot, core_s, core)

    def spread(slot):
        pl.when(z < last)(lambda: up(slot).start())
        pl.when(z > 0)(lambda: down(slot).start())
        over(slot).start()

    spread(me)
    below_k = remote(k_ref, ka, win_s.at[0], win_r.at[0], me + 1)
    below_v = remote(v_ref, va, win_s.at[1], win_r.at[1], me + 1)
    above_k = remote(k_ref, kb, win_s.at[2], win_r.at[2], me - 1)
    above_v = remote(v_ref, vb, win_s.at[3], win_r.at[3], me - 1)

    @pl.when(me < n - 1)
    def _():
        below_k.start()
        below_v.start()

    @pl.when(me > 0)
    def _():
        above_k.start()
        above_v.start()

    hop(side, core_s, core).wait_recv()
    spread(side)
    for s in range(1, depth):
        for flip in range(2):
            row = y + flip * (1 - 2 * y)

            @pl.when(z - s >= 0)
            def _():
                slot = 4 * (z - s) + 2 * row + c
                over(slot).wait_recv()
                pl.when(z < last)(lambda: up(slot).start())
                over(slot).start()

            @pl.when(z + s <= last)
            def _():
                slot = 4 * (z + s) + 2 * row + c
                over(slot).wait_recv()
                pl.when(z > 0)(lambda: down(slot).start())
                over(slot).start()

    for k in range(half):
        over(2 * k + 1 - c).wait_recv()

    @pl.when(me > 0)
    def _():
        below_k.wait_recv()
        below_v.wait_recv()

    @pl.when(me < n - 1)
    def _():
        above_k.wait_recv()
        above_v.wait_recv()

    to_side.wait_send()
    for k in range(half):
        over(2 * k + c).wait_send()
        pl.when(jnp.logical_and(z < last, k // 2 <= z))(lambda: up(2 * k + c).wait_send())
        pl.when(jnp.logical_and(z > 0, k // 2 >= z))(lambda: down(2 * k + c).wait_send())

    @pl.when(me < n - 1)
    def _():
        below_k.wait_send()
        below_v.wait_send()

    @pl.when(me > 0)
    def _():
        above_k.wait_send()
        above_v.wait_send()


def attend_kernel(
    n,
    counts_ref,
    cols_ref,
    rows_ref,
    q_ref,
    do_ref,
    k_ref,
    v_ref,
    ka,
    va,
    kb,
    vb,
    panel,
    attn_ref,
    qgrad_ref,
    g_above,
    g_own,
    g_below,
    g_land,
    k_all,
    v_all,
    k_t,
    v_t,
    q_s,
    do_m,
    q_t,
    do_t,
    o_t,
    dq_t,
    bias,
):
    me = lax.axis_index("prow")
    k_all[0:ROWS] = ka[...]
    k_all[ROWS : 2 * ROWS] = k_ref[...]
    k_all[2 * ROWS : 3 * ROWS] = kb[...]
    v_all[0:ROWS] = va[...]
    v_all[ROWS : 2 * ROWS] = v_ref[...]
    v_all[2 * ROWS : 3 * ROWS] = vb[...]
    pos = lax.broadcasted_iota(jnp.int32, (BLK, ROWS), 0)
    qcol = lax.broadcasted_iota(jnp.int32, (BLK, ROWS), 1) // BLK
    for a in range(3):
        row = me + a - 1
        inside = jnp.logical_and(row >= 0, row < n)
        safe = jnp.clip(row, 0, n - 1)
        for b in range(PC):
            count = jnp.where(inside, counts_ref[safe, b], 0)
            ok = (pos < count) & (qcol >= b - 1) & (qcol <= b + 1)
            base = a * ROWS + b * BLK
            bias[base : base + BLK] = jnp.where(ok, 0.0, masked_score)
    for j in range(NLAND):
        row = rows_ref[0, j]
        count = counts_ref[row, cols_ref[row]]
        base = 3 * ROWS + j * BLK
        bias[base : base + BLK] = jnp.where(pos < count, 0.0, masked_score)
        k_all[base : base + BLK] = panel[row, :, :WIDTH]
        v_all[base : base + BLK] = panel[row, :, WIDTH:]
    k_t[...] = k_all[...].T
    v_t[...] = v_all[...].T
    q_s[...] = q_ref[...] * 0.125
    tpos = lax.broadcasted_iota(jnp.int32, (BLK, WIDTH), 0)
    lane = lax.broadcasted_iota(jnp.int32, (1, ROWS), 1)
    own_valid = jnp.zeros((1, ROWS), jnp.bool_)
    for b in range(PC):
        count = counts_ref[me, b]
        own_valid = own_valid | ((lane >= b * BLK) & (lane < b * BLK + count))
        part = do_ref[b * BLK : (b + 1) * BLK].astype(F32)
        do_m[b * BLK : (b + 1) * BLK] = jnp.where(tpos < count, part, 0.0).astype(BF16)
    q_t[...] = q_s[...].T
    do_t[...] = do_m[...].T
    g_land[NLAND] = jnp.zeros((BLK, 2 * WIDTH), BF16)

    def pair(p, carry):
        cols = pl.ds(pl.multiple_of(p * 128, 128), 128)
        vcols = pl.ds(pl.multiple_of(WIDTH + p * 128, 128), 128)
        k2 = k_all[:, cols]
        v2 = v_all[:, cols]
        q2 = q_s[:, cols]
        do2 = do_m[:, cols]
        zero = jnp.zeros((HD, ROWS), BF16)
        left = lax.broadcasted_iota(jnp.int32, (ROWS, 128), 1) < HD
        dk2 = None
        dv2 = None
        for h in range(2):
            rows = pl.ds(pl.multiple_of(p * 128 + h * HD, HD), HD)
            qt = q_t[rows, :]
            dot_t = do_t[rows, :]
            qt_w = jnp.concatenate([qt, zero] if h == 0 else [zero, qt], axis=0)
            dot_w = jnp.concatenate([dot_t, zero] if h == 0 else [zero, dot_t], axis=0)
            keep = left if h == 0 else jnp.logical_not(left)
            q_w = jnp.where(keep, q2.astype(F32), 0.0).astype(BF16)
            do_w = jnp.where(keep, do2.astype(F32), 0.0).astype(BF16)
            s = dot(k2, qt_w) + bias[...]
            top = jnp.max(s, axis=0, keepdims=True)
            e = jnp.exp(s - top)
            prob = e * (1.0 / jnp.sum(e, axis=0, keepdims=True))
            low = prob.astype(BF16)
            mixed = dot(v_t[rows, :], low)
            o_t[rows, :] = jnp.where(own_valid, mixed, 0.0)
            delta = jnp.sum(dot_t.astype(F32) * mixed, axis=0, keepdims=True)
            dprob = dot(v2, dot_w)
            ds = (prob * (dprob - delta)).astype(BF16)
            dq_t[rows, :] = dot(k_t[rows, :], ds) * 0.125
            dk = dot(ds, q_w)
            dv = dot(low, do_w)
            dk2 = dk if dk2 is None else dk2 + dk
            dv2 = dv if dv2 is None else dv2 + dv
        for part, where in ((dk2, cols), (dv2, vcols)):
            g_above[:, where] = part[0:ROWS].astype(BF16)
            g_own[:, where] = part[ROWS : 2 * ROWS]
            g_below[:, where] = part[2 * ROWS : 3 * ROWS].astype(BF16)
            for j in range(NLAND):
                base = 3 * ROWS + j * BLK
                g_land[j, :, where] = part[base : base + BLK].astype(BF16)
        return carry

    lax.fori_loop(0, HEADS // 2, pair, 0)
    attn_ref[...] = o_t[...].T.astype(BF16)
    qgrad_ref[...] = dq_t[...].T.astype(BF16)


def reduce_kernel(
    n,
    inv_ref,
    hit_ref,
    g_above,
    g_own,
    g_below,
    g_land,
    kgrad_ref,
    vgrad_ref,
    from_below,
    from_above,
    core_tx,
    core_rx,
    acc,
    up_rx,
    dn_rx,
    side_rx,
    core_s,
    core_r,
    hop_s,
    up_r,
    dn_r,
    side_s,
    side_r,
    win_s,
    win_r,
):
    me, z, y, c, core, side = position(n)
    depth = n // 4
    last = depth - 1
    greet(n)

    def over(k):
        return remote(core_tx.at[k], core_rx.at[k], core_s.at[k], core_r.at[k], core)

    def up(k):
        return remote(acc.at[k], up_rx.at[k], hop_s.at[k], up_r.at[k], me + 4)

    def down(k):
        return remote(acc.at[k], dn_rx.at[k], hop_s.at[k], dn_r.at[k], me - 4)

    def give(k):
        core_tx[k] = g_land[inv_ref[2 * k + 1 - c]]
        over(k).start()

    for s in range(depth - 1, -1, -1):
        for row in range(2):
            pl.when(z + s <= last)(lambda: give(2 * (z + s) + row))
            if s > 0:
                pl.when(z - s >= 0)(lambda: give(2 * (z - s) + row))
    to_above = remote(g_above, from_below, win_s.at[0], win_r.at[0], me - 1)
    to_below = remote(g_below, from_above, win_s.at[1], win_r.at[1], me + 1)
    pl.when(me > 0)(lambda: to_above.start())
    pl.when(me < n - 1)(lambda: to_below.start())

    def mine(k):
        over(k).wait_recv()
        return core_rx[k].astype(F32) + g_land[inv_ref[2 * k + c]].astype(F32)

    for s in range(depth - 1, 0, -1):
        for row in range(2):

            @pl.when(z + s <= last)
            def _():
                k = 2 * (z + s) + row
                total = mine(k)

                @pl.when(z > 0)
                def _():
                    up(k).wait_recv()
                    acc[k] = (total + up_rx[k].astype(F32)).astype(BF16)

                @pl.when(z == 0)
                def _():
                    acc[k] = total.astype(BF16)

                up(k).start()

            @pl.when(z - s >= 0)
            def _():
                k = 2 * (z - s) + row
                total = mine(k)

                @pl.when(z < last)
                def _():
                    down(k).wait_recv()
                    acc[k] = (total + dn_rx[k].astype(F32)).astype(BF16)

                @pl.when(z == last)
                def _():
                    acc[k] = total.astype(BF16)

                down(k).start()

    def arrived(k):
        pl.when(z > 0)(lambda: up(k).wait_recv())
        pl.when(z < last)(lambda: down(k).wait_recv())
        low = jnp.where(z > 0, up_rx[k].astype(F32), 0.0)
        high = jnp.where(z < last, dn_rx[k].astype(F32), 0.0)
        return mine(k) + low + high

    @pl.when(z == 0)
    def _():
        for row in range(2):
            up_rx[row] = jnp.zeros((BLK, 2 * WIDTH), BF16)

    @pl.when(z == last)
    def _():
        for row in range(2):
            dn_rx[2 * last + row] = jnp.zeros((BLK, 2 * WIDTH), BF16)

    theirs = 2 * z + 1 - y
    acc[theirs] = arrived(theirs).astype(BF16)
    to_side = remote(acc.at[theirs], side_rx, side_s.at[0], side_r.at[0], side)
    to_side.start()
    total = arrived(2 * z + y)

    @pl.when(me == n - 1)
    def _():
        from_below[...] = jnp.zeros_like(from_below)

    @pl.when(me == 0)
    def _():
        from_above[...] = jnp.zeros_like(from_above)

    pl.when(me < n - 1)(lambda: to_above.wait_recv())
    pl.when(me > 0)(lambda: to_below.wait_recv())
    to_side.wait_recv()
    total = total + side_rx[...].astype(F32)
    for b in range(PC):
        span = pl.ds(b * BLK, BLK)
        part = (
            g_own[span, :]
            + from_above[span, :].astype(F32)
            + from_below[span, :].astype(F32)
            + jnp.where(hit_ref[0] == b, total, 0.0)
        ).astype(BF16)
        kgrad_ref[span, :] = part[:, :WIDTH]
        vgrad_ref[span, :] = part[:, WIDTH:]
    to_side.wait_send()
    pl.when(me > 0)(lambda: to_above.wait_send())
    pl.when(me < n - 1)(lambda: to_below.wait_send())
    for k in range(n // 2):
        over(k).wait_send()
        pl.when(k // 2 > z)(lambda: up(k).wait_send())
        pl.when(k // 2 < z)(lambda: down(k).wait_send())


VM = pl.BlockSpec(memory_space=pltpu.VMEM)
SM = pl.BlockSpec(memory_space=pltpu.SMEM)
DMA = pltpu.SemaphoreType.DMA


def shape(dims, dtype):
    return jax.ShapeDtypeStruct(dims, dtype)


def per_device(n, queries, keys, values, out_grad, valid_counts, landmark_cols, landmark_rows):
    half = n // 2
    block_rows = (PC, BLK, WIDTH)
    k4 = keys.reshape(block_rows)
    v4 = values.reshape(block_rows)
    ka, va, kb, vb, panel = pl.pallas_call(
        functools.partial(gather_kernel, n),
        out_shape=[shape(block_rows, BF16)] * 4 + [shape((n, BLK, 2 * WIDTH), BF16)],
        in_specs=[SM, VM, VM],
        out_specs=[VM] * 5,
        scratch_shapes=[
            DMA((n,)),
            DMA((half,)),
            DMA((half,)),
            DMA((half,)),
            DMA((1,)),
            DMA((4,)),
            DMA((4,)),
        ],
        compiler_params=pltpu.CompilerParams(
            collective_id=0, has_side_effects=True, vmem_limit_bytes=VMEM_LIMIT
        ),
    )(landmark_cols, k4, v4)
    flat = (ROWS, WIDTH)
    attn_out, query_grad, g_above, g_own, g_below, g_land = pl.pallas_call(
        functools.partial(attend_kernel, n),
        out_shape=[
            shape(flat, BF16),
            shape(flat, BF16),
            shape((ROWS, 2 * WIDTH), BF16),
            shape((ROWS, 2 * WIDTH), F32),
            shape((ROWS, 2 * WIDTH), BF16),
            shape((NLAND + 1, BLK, 2 * WIDTH), BF16),
        ],
        in_specs=[SM] * 3 + [VM] * 9,
        out_specs=[VM] * 6,
        scratch_shapes=[
            pltpu.VMEM((KEYS, WIDTH), BF16),
            pltpu.VMEM((KEYS, WIDTH), BF16),
            pltpu.VMEM((WIDTH, KEYS), BF16),
            pltpu.VMEM((WIDTH, KEYS), BF16),
            pltpu.VMEM((ROWS, WIDTH), BF16),
            pltpu.VMEM((ROWS, WIDTH), BF16),
            pltpu.VMEM((WIDTH, ROWS), BF16),
            pltpu.VMEM((WIDTH, ROWS), BF16),
            pltpu.VMEM((WIDTH, ROWS), F32),
            pltpu.VMEM((WIDTH, ROWS), F32),
            pltpu.VMEM((KEYS, ROWS), F32),
        ],
        compiler_params=pltpu.CompilerParams(vmem_limit_bytes=VMEM_LIMIT),
    )(
        valid_counts,
        landmark_cols,
        landmark_rows,
        queries,
        out_grad,
        keys,
        values,
        ka.reshape(flat),
        va.reshape(flat),
        kb.reshape(flat),
        vb.reshape(flat),
        panel,
    )
    match = landmark_rows[0][None, :] == jnp.arange(n, dtype=jnp.int32)[:, None]
    slots = jnp.arange(NLAND, dtype=jnp.int32)[None, :] - NLAND
    inverse = NLAND + jnp.sum(jnp.where(match, slots, 0), axis=1)
    hit = lax.dynamic_slice_in_dim(landmark_cols, lax.axis_index("prow"), 1, 0)
    block = (BLK, 2 * WIDTH)
    many = pltpu.VMEM((half,) + block, BF16)
    key_grad, value_grad = pl.pallas_call(
        functools.partial(reduce_kernel, n),
        out_shape=[shape(flat, BF16)] * 2,
        in_specs=[SM] * 2 + [VM] * 4,
        out_specs=[VM] * 2,
        scratch_shapes=[
            pltpu.VMEM((ROWS, 2 * WIDTH), BF16),
            pltpu.VMEM((ROWS, 2 * WIDTH), BF16),
            many,
            many,
            many,
            many,
            many,
            pltpu.VMEM(block, BF16),
            DMA((half,)),
            DMA((half,)),
            DMA((half,)),
            DMA((half,)),
            DMA((half,)),
            DMA((1,)),
            DMA((1,)),
            DMA((2,)),
            DMA((2,)),
        ],
        compiler_params=pltpu.CompilerParams(
            collective_id=1, has_side_effects=True, vmem_limit_bytes=VMEM_LIMIT
        ),
    )(inverse, hit, g_above, g_own, g_below, g_land)
    return attn_out, query_grad, key_grad, value_grad


def solution(mesh):
    n = mesh.shape["prow"]
    tokens = P(("chars", "prow"), None)
    return jax.shard_map(
        functools.partial(per_device, n),
        mesh=mesh,
        in_specs=(tokens, tokens, tokens, tokens, P("chars", None), P("chars"), tokens),
        out_specs=(tokens, tokens, tokens, tokens),
        check_vma=False,
    )
```

time: 193 us -> 91.6 us (0.47)
  the two profiles are of different devices: /device:TPU:1 before, /device:TPU:0 now
where the time goes in v1:
time: 91.6 us; the launch traced here: 91.3 us
  Pallas kernels  84.8 us (93%)
  local copies, waits for them, and re-layouts  5.29 us (6%)
    pallas_call x1, Pallas kernels, per_device(): pl.pallas_call(functools.partial(reduce_kernel, n), out_shape=[shape(flat...  35.1 us
    pallas_call x1, Pallas kernels, per_device(): pl.pallas_call(functools.partial(gather_kernel, n), out_shape=[shape(bloc...  32.3 us
    pallas_call x1, Pallas kernels, per_device(): pl.pallas_call(functools.partial(attend_kernel, n), out_shape=[shape(flat...  17.5 us
    unnamed x7, local copies, waits for them, and re-layouts  4.7 us

profile of v1, /device:TPU:0, one launch (start us, length us, event | category | flops | bytes accessed | tf_op | source)
XLA Modules:
  0.0 91.3 jit_solution(18076869864835249816)
XLA Ops:
  0.6 32.3 %shard_map.102 = (bf16[4,64,512]{2,1,0:T(8,128)(2,1)}, bf16[4,64,512]{2,1,0:T(8,128)(2,1)}, bf16[4,64,512]{2,1,0:T(8,128)(2,1)}, bf16[4,64,512]{2,1,0:T(8,128)(2,1)}, bf16[16,64,1024]{2,1,0:T(8,128)(2,1)}) custom-call(s32[16]{0:T(128)} %cols_ref.3, bf16[4,64,512]{2,1,0:T(8,128)(2,1)} %bitcast.7, bf16[4,64,512]{2,1,0:T(8,128)(2,1)} %bitcast.8), custom_call_target="tpu_custom_call" | custom-call | tf_op jit(solution)/shard_map/pallas_call | solution.py:480
  32.9 1.4 %copy.12.counts_ref = s32[16,4]{1,0:T(8,128)} copy(s32[16,4]{0,1:T(4,128)} %param.11) | data formatting | bytes 512 | tf_op args[4]
  34.2 0.0 copy-start
  34.3 0.0 copy-start.1
  34.3 17.5 %shard_map.103 = (bf16[256,512]{1,0:T(8,128)(2,1)}, bf16[256,512]{1,0:T(8,128)(2,1)}, bf16[256,1024]{1,0:T(8,128)(2,1)}, f32[256,1024]{1,0:T(8,128)}, bf16[256,1...) custom-call(s32[16,4]{1,0:T(8,128)} %copy.12.counts_ref, s32[16]{0:T(128)} %cols_ref.3, s32[1,4]{1,0:T(1,128)} %rows_ref.1, ...), custom_call_target="tpu_custom_call" | custom-call | tf_op jit(solution)/shard_map/pallas_call | solution.py:499
  51.7 0.0 copy-done
  51.7 0.6 dynamic_slice.3.hit_ref
  52.3 0.0 copy-done.1
  52.3 0.1 select_reduce_fusion
  52.4 0.5 broadcast_add_fusion.inv_ref
  52.9 35.1 %shard_map.104 = (bf16[256,512]{1,0:T(8,128)(2,1)}, bf16[256,512]{1,0:T(8,128)(2,1)}) custom-call(s32[16]{0:T(128)} %broadcast_add_fusion.inv_ref, s32[1]{0:T(128)} %dynamic_slice.3.hit_ref, bf16[256,1024]{1,0:T(8,128)(2,1)} %get-tuple-element.24.g_above, f32[256,1024]{1,0:T(8,128)} %get-tuple-element.25.g_own, bf16[256,1024]{1,0:T(8,128)(2,1)} %get-tuple-element.26.g_below, ...), custom_call_target="tpu_custom_call" | custom-call | tf_op jit(solution)/shard_map/pallas_call | solution.py:545
  88.0 1.7 %copy.15 = bf16[256,512]{1,0:T(8,128)(2,1)} copy(bf16[256,512]{1,0:T(8,128)(2,1)} %get-tuple-element.36) | data formatting | bytes 524288
  89.7 1.7 %copy.16 = bf16[256,512]{1,0:T(8,128)(2,1)} copy(bf16[256,512]{1,0:T(8,128)(2,1)} %get-tuple-element.37) | data formatting | bytes 524288
  (1 shorter events, 0.0 us)
Async XLA Ops:
  34.2 17.5 %copy-start = (s32[16]{0:T(128)S(1)}, s32[16]{0:T(128)}, u32[]{:S(2)}) copy-start(s32[16]{0:T(128)} %cols_ref.3) | copy-start | bytes 196
  34.3 18.1 %copy-start.1 = (s32[1,4]{1,0:T(1,128)S(1)}, s32[1,4]{1,0:T(1,128)}, u32[]{:S(2)}) copy-start(s32[1,4]{1,0:T(1,128)} %rows_ref.1) | copy-start | bytes 52

commit v2 on v1

v2 whole, which is shorter than its diff:
```python
import functools

import jax
import jax.numpy as jnp
from jax import lax
from jax.experimental import pallas as pl
from jax.experimental.pallas import tpu as pltpu
from jax.sharding import PartitionSpec as P

HEADS = 8
HD = 64
BLK = 64
NLAND = 4
PC = 4
WIDTH = HEADS * HD
ROWS = PC * BLK
KEYS = 3 * ROWS + NLAND * BLK
F32 = jnp.float32
BF16 = jnp.bfloat16
MESH = pl.DeviceIdType.MESH
masked_score = -1e30
WIN = 3 * ROWS
VMEM_LIMIT = 60 * 1024 * 1024


def dot(a, b):
    return lax.dot_general(a, b, (((1,), (0,)), ((), ())), preferred_element_type=F32)


def remote(src, dst, send, recv, device):
    return pltpu.make_async_remote_copy(
        src_ref=src,
        dst_ref=dst,
        send_sem=send,
        recv_sem=recv,
        device_id={"prow": device},
        device_id_type=MESH,
    )


def position(n):
    me = lax.axis_index("prow")
    z, y, c = me // 4, (me // 2) % 2, me % 2
    core = me + 1 - 2 * c
    side = me + 2 - 4 * y
    return me, z, y, c, core, side


def greet(n):
    me, z, y, c, core, side = position(n)
    last = n // 4 - 1
    other = me + 2 * c - 1
    has_other = jnp.logical_and(other >= 0, other < n)
    barrier = pltpu.get_barrier_semaphore()

    def signal(device):
        pl.semaphore_signal(barrier, inc=1, device_id={"prow": device}, device_id_type=MESH)

    signal(core)
    signal(side)
    pl.when(z > 0)(lambda: signal(me - 4))
    pl.when(z < last)(lambda: signal(me + 4))
    pl.when(has_other)(lambda: signal(other))
    count = (
        2
        + jnp.where(z > 0, 1, 0)
        + jnp.where(z < last, 1, 0)
        + jnp.where(has_other, 1, 0)
    )
    pl.semaphore_wait(barrier, count)


def fused_kernel(
    n,
    cols_ref,
    rows_ref,
    counts_ref,
    q_ref,
    k_ref,
    v_ref,
    do_ref,
    attn_ref,
    qgrad_ref,
    kgrad_ref,
    vgrad_ref,
    panel,
    ka,
    va,
    kb,
    vb,
    k_all,
    v_all,
    k_t,
    v_t,
    q_s,
    do_m,
    q_t,
    do_t,
    o_t,
    dq_t,
    bias,
    e_win,
    top_win,
    sum_win,
    low_win,
    ds_win,
    g_above,
    g_own,
    g_below,
    from_below,
    from_above,
    g_land,
    core_tx,
    core_rx,
    up_rx,
    dn_rx,
    side_rx,
    total_ref,
    recv,
    up_s,
    dn_s,
    core_s,
    side_s,
    win_s,
    win_r,
    r_core_s,
    r_core_r,
    r_hop_s,
    r_up_r,
    r_dn_r,
    r_side_s,
    r_side_r,
    r_win_s,
    r_win_r,
):
    me, z, y, c, core, side = position(n)
    depth = n // 4
    last = depth - 1
    half = n // 2
    own_col = cols_ref[me]
    panel[me, :, :WIDTH] = k_ref[own_col]
    panel[me, :, WIDTH:] = v_ref[own_col]

    @pl.when(me == 0)
    def _():
        ka[...] = jnp.zeros_like(ka)
        va[...] = jnp.zeros_like(va)
        from_above[...] = jnp.zeros_like(from_above)

    @pl.when(me == n - 1)
    def _():
        kb[...] = jnp.zeros_like(kb)
        vb[...] = jnp.zeros_like(vb)
        from_below[...] = jnp.zeros_like(from_below)

    greet(n)

    def hop(slot, sems, device):
        return remote(panel.at[slot], panel.at[slot], sems.at[slot // 2], recv.at[slot], device)

    def up(slot):
        return hop(slot, up_s, me + 4)

    def down(slot):
        return hop(slot, dn_s, me - 4)

    def over(slot):
        return hop(slot, core_s, core)

    def spread(slot):
        pl.when(z < last)(lambda: up(slot).start())
        pl.when(z > 0)(lambda: down(slot).start())
        over(slot).start()

    to_side = remote(panel.at[me], panel.at[me], side_s.at[0], recv.at[me], side)
    to_side.start()
    spread(me)
    below_k = remote(k_ref, ka, win_s.at[0], win_r.at[0], me + 1)
    below_v = remote(v_ref, va, win_s.at[1], win_r.at[1], me + 1)
    above_k = remote(k_ref, kb, win_s.at[2], win_r.at[2], me - 1)
    above_v = remote(v_ref, vb, win_s.at[3], win_r.at[3], me - 1)

    @pl.when(me < n - 1)
    def _():
        below_k.start()

    @pl.when(me > 0)
    def _():
        above_k.start()

    @pl.when(me < n - 1)
    def _():
        below_v.start()

    @pl.when(me > 0)
    def _():
        above_v.start()

    pos = lax.broadcasted_iota(jnp.int32, (BLK, ROWS), 0)
    qcol = lax.broadcasted_iota(jnp.int32, (BLK, ROWS), 1) // BLK

    for a in range(3):
        row = me + a - 1
        inside = jnp.logical_and(row >= 0, row < n)
        safe = jnp.clip(row, 0, n - 1)
        for b in range(PC):
            count = jnp.where(inside, counts_ref[safe, b], 0)
            ok = (pos < count) & (qcol >= b - 1) & (qcol <= b + 1)
            base = a * ROWS + b * BLK
            bias[base : base + BLK] = jnp.where(ok, 0.0, masked_score)
    for j in range(NLAND):
        row = rows_ref[0, j]
        count = counts_ref[row, cols_ref[row]]
        base = WIN + j * BLK
        bias[base : base + BLK] = jnp.where(pos < count, 0.0, masked_score)
    q_s[...] = q_ref[...] * 0.125
    tpos = lax.broadcasted_iota(jnp.int32, (BLK, WIDTH), 0)
    for b in range(PC):
        part = do_ref[b * BLK : (b + 1) * BLK].astype(F32)
        do_m[b * BLK : (b + 1) * BLK] = jnp.where(tpos < counts_ref[me, b], part, 0.0).astype(BF16)
    q_t[...] = q_s[...].T
    do_t[...] = do_m[...].T
    for g in range(2):
        g_land[g, NLAND] = jnp.zeros((BLK, WIDTH), BF16)

    def own_part(lo, hi, k_rows, v_rows):
        k_rows = k_rows.reshape(hi - lo, WIDTH)
        v_rows = v_rows.reshape(hi - lo, WIDTH)
        k_all[lo:hi] = k_rows
        v_all[lo:hi] = v_rows
        k_t[:, lo:hi] = k_rows.T
        v_t[:, lo:hi] = v_rows.T

    own_part(ROWS, 2 * ROWS, k_ref[...], v_ref[...])

    hop(side, core_s, core).wait_recv()
    spread(side)

    def chain(s):
        for flip in range(2):
            row = y + flip * (1 - 2 * y)

            @pl.when(z - s >= 0)
            def _():
                slot = 4 * (z - s) + 2 * row + c
                over(slot).wait_recv()
                pl.when(z < last)(lambda: up(slot).start())
                over(slot).start()

            @pl.when(z + s <= last)
            def _():
                slot = 4 * (z + s) + 2 * row + c
                over(slot).wait_recv()
                pl.when(z > 0)(lambda: down(slot).start())
                over(slot).start()

    for s in range(1, last):
        chain(s)

    @pl.when(me > 0)
    def _():
        below_k.wait_recv()
        below_v.wait_recv()

    @pl.when(me < n - 1)
    def _():
        above_k.wait_recv()
        above_v.wait_recv()

    own_part(0, ROWS, ka[...], va[...])
    own_part(2 * ROWS, WIN, kb[...], vb[...])
    zero = jnp.zeros((HD, ROWS), BF16)

    def padded(rows_t, h):
        return jnp.concatenate([rows_t, zero] if h == 0 else [zero, rows_t], axis=0)

    def head_rows(p, h):
        return pl.ds(pl.multiple_of(p * 128 + h * HD, HD), HD)

    def pair_cols(p):
        return pl.ds(pl.multiple_of(p * 128, 128), 128)

    def window_scores(p, carry):
        k2 = k_all[0:WIN, pair_cols(p)]
        for h in range(2):
            s = dot(k2, padded(q_t[head_rows(p, h), :], h)) + bias[0:WIN]
            top = jnp.max(s, axis=0, keepdims=True)
            e = jnp.exp(s - top)
            e_win[2 * p + h] = e
            top_win[2 * p + h] = top
            sum_win[2 * p + h] = jnp.sum(e, axis=0, keepdims=True)
        return carry

    lax.fori_loop(0, HEADS // 2, window_scores, 0)
    if last > 0:
        chain(last)
    for k in range(half):
        over(2 * k + 1 - c).wait_recv()
    for j in range(NLAND):
        row = rows_ref[0, j]
        block = panel[row]
        own_part(WIN + j * BLK, WIN + (j + 1) * BLK, block[:, :WIDTH], block[:, WIDTH:])

    left = lax.broadcasted_iota(jnp.int32, (ROWS, 128), 1) < HD

    def halved(block, h):
        keep = left if h == 0 else jnp.logical_not(left)
        return jnp.where(keep, block.astype(F32), 0.0).astype(BF16)

    def landmarks(g, i):
        p = 2 * g + i
        k2 = k_all[WIN:KEYS, pair_cols(p)]
        v2 = v_all[:, pair_cols(p)]
        q2 = q_s[:, pair_cols(p)]
        do2 = do_m[:, pair_cols(p)]
        dk2 = 0.0
        dv2 = 0.0
        for h in range(2):
            rows = head_rows(p, h)
            head = 2 * p + h
            s = dot(k2, padded(q_t[rows, :], h)) + bias[WIN:KEYS]
            top_w = top_win[head]
            top = jnp.maximum(jnp.max(s, axis=0, keepdims=True), top_w)
            e = jnp.exp(s - top)
            scale_w = jnp.exp(top_w - top)
            inv_total = 1.0 / (jnp.sum(e, axis=0, keepdims=True) + sum_win[head] * scale_w)
            prob_l = e * inv_total
            prob_w = e_win[head] * (scale_w * inv_total)
            low_l = prob_l.astype(BF16)
            low_w = prob_w.astype(BF16)
            low_win[head] = low_w
            mixed = dot(v_t[rows, 0:WIN], low_w) + dot(v_t[rows, WIN:KEYS], low_l)
            o_t[rows, :] = mixed
            dot_t = do_t[rows, :]
            delta = jnp.sum(dot_t.astype(F32) * mixed, axis=0, keepdims=True)
            dot_w = padded(dot_t, h)
            ds_l = (prob_l * (dot(v2[WIN:KEYS], dot_w) - delta)).astype(BF16)
            ds_w = (prob_w * (dot(v2[0:WIN], dot_w) - delta)).astype(BF16)
            ds_win[head] = ds_w
            dq_t[rows, :] = (dot(k_t[rows, 0:WIN], ds_w) + dot(k_t[rows, WIN:KEYS], ds_l)) * 0.125
            dk2 = dk2 + dot(ds_l, halved(q2, h))
            dv2 = dv2 + dot(low_l, halved(do2, h))
        for j in range(NLAND):
            span = slice(j * BLK, (j + 1) * BLK)
            g_land[g, j, :, i * 128 : (i + 1) * 128] = dk2[span].astype(BF16)
            g_land[g, j, :, 256 + i * 128 : 256 + (i + 1) * 128] = dv2[span].astype(BF16)

    def slot_of(device):
        found = NLAND
        for j in range(NLAND):
            found = jnp.where(rows_ref[0, j] == device, j, found)
        return found

    def r_over(g, k):
        return remote(
            core_tx.at[g, k], core_rx.at[g, k], r_core_s.at[g, k], r_core_r.at[g, k], core
        )

    def r_up(g, k):
        return remote(core_rx.at[g, k], up_rx.at[g, k], r_hop_s.at[g, k], r_up_r.at[g, k], me + 4)

    def r_down(g, k):
        return remote(core_rx.at[g, k], dn_rx.at[g, k], r_hop_s.at[g, k], r_dn_r.at[g, k], me - 4)

    def give(g, k):
        core_tx[g, k] = g_land[g, slot_of(2 * k + 1 - c)]
        r_over(g, k).start()

    def give_all(g):
        for s in range(last, -1, -1):
            for row in range(2):
                pl.when(z + s <= last)(lambda: give(g, 2 * (z + s) + row))
                if s > 0:
                    pl.when(z - s >= 0)(lambda: give(g, 2 * (z - s) + row))

    def mine(g, k):
        r_over(g, k).wait_recv()
        return core_rx[g, k].astype(F32) + g_land[g, slot_of(2 * k + c)].astype(F32)

    def reduce_step(g, s):
        for row in range(2):

            @pl.when(z + s <= last)
            def _():
                k = 2 * (z + s) + row
                total = mine(g, k)

                @pl.when(z > 0)
                def _():
                    r_up(g, k).wait_recv()
                    core_rx[g, k] = (total + up_rx[g, k].astype(F32)).astype(BF16)

                @pl.when(z == 0)
                def _():
                    core_rx[g, k] = total.astype(BF16)

                r_up(g, k).start()

            @pl.when(z - s >= 0)
            def _():
                k = 2 * (z - s) + row
                total = mine(g, k)

                @pl.when(z < last)
                def _():
                    r_down(g, k).wait_recv()
                    core_rx[g, k] = (total + dn_rx[g, k].astype(F32)).astype(BF16)

                @pl.when(z == last)
                def _():
                    core_rx[g, k] = total.astype(BF16)

                r_down(g, k).start()

    def to_above(p):
        return remote(g_above.at[p], from_below.at[p], r_win_s.at[0, p], r_win_r.at[0, p], me - 1)

    def to_below(p):
        return remote(g_below.at[p], from_above.at[p], r_win_s.at[1, p], r_win_r.at[1, p], me + 1)

    def window_grads(p):
        q2 = q_s[:, p * 128 : (p + 1) * 128]
        do2 = do_m[:, p * 128 : (p + 1) * 128]
        dk2 = dot(ds_win[2 * p], halved(q2, 0)) + dot(ds_win[2 * p + 1], halved(q2, 1))
        dv2 = dot(low_win[2 * p], halved(do2, 0)) + dot(low_win[2 * p + 1], halved(do2, 1))
        for part, cols in ((dk2, slice(0, 128)), (dv2, slice(128, 256))):
            g_above[p, :, cols] = part[0:ROWS].astype(BF16)
            g_own[p, :, cols] = part[ROWS : 2 * ROWS]
            g_below[p, :, cols] = part[2 * ROWS : WIN].astype(BF16)
        pl.when(me > 0)(lambda: to_above(p).start())
        pl.when(me < n - 1)(lambda: to_below(p).start())

    for g in range(2):
        for i in range(2):
            landmarks(g, i)
        give_all(g)
    steps = [(g, s) for s in range(last, 0, -1) for g in range(2)]
    for at in range(max(len(steps), HEADS // 2)):
        if at < HEADS // 2:
            window_grads(at)
        if at < len(steps):
            reduce_step(*steps[at])

    lane = lax.broadcasted_iota(jnp.int32, (1, ROWS), 1)
    own_valid = jnp.zeros((1, ROWS), jnp.bool_)
    for b in range(PC):
        own_valid = own_valid | ((lane >= b * BLK) & (lane < b * BLK + counts_ref[me, b]))
    attn_ref[...] = jnp.where(own_valid, o_t[...], 0.0).T.astype(BF16)
    qgrad_ref[...] = dq_t[...].T.astype(BF16)

    @pl.when(z == 0)
    def _():
        for g in range(2):
            for row in range(2):
                up_rx[g, row] = jnp.zeros((BLK, WIDTH), BF16)

    @pl.when(z == last)
    def _():
        for g in range(2):
            for row in range(2):
                dn_rx[g, 2 * last + row] = jnp.zeros((BLK, WIDTH), BF16)

    def arrived(g, k):
        pl.when(z > 0)(lambda: r_up(g, k).wait_recv())
        pl.when(z < last)(lambda: r_down(g, k).wait_recv())
        return mine(g, k) + up_rx[g, k].astype(F32) + dn_rx[g, k].astype(F32)

    theirs = 2 * z + 1 - y

    def r_side(g):
        return remote(
            core_rx.at[g, theirs], side_rx.at[g], r_side_s.at[g], r_side_r.at[g], side
        )

    for g in range(2):
        core_rx[g, theirs] = arrived(g, theirs).astype(BF16)
        r_side(g).start()
    for g in range(2):
        total_ref[g] = arrived(g, 2 * z + y)
    for p in range(HEADS // 2):
        pl.when(me < n - 1)(lambda: to_above(p).wait_recv())
        pl.when(me > 0)(lambda: to_below(p).wait_recv())
    for g in range(2):
        r_side(g).wait_recv()
        total_ref[g] = total_ref[g] + side_rx[g].astype(F32)
    for p in range(HEADS // 2):
        g, i = p // 2, p % 2
        for b in range(PC):
            span = slice(b * BLK, (b + 1) * BLK)
            hit = own_col == b
            for out, cols, base in (
                (kgrad_ref, slice(0, 128), i * 128),
                (vgrad_ref, slice(128, 256), 256 + i * 128),
            ):
                out[span, p * 128 : (p + 1) * 128] = (
                    g_own[p, span, cols]
                    + from_above[p, span, cols].astype(F32)
                    + from_below[p, span, cols].astype(F32)
                    + jnp.where(hit, total_ref[g, :, base : base + 128], 0.0)
                ).astype(BF16)

    to_side.wait_send()
    for k in range(half):
        slot = 2 * k + c
        over(slot).wait_send()
        pl.when(jnp.logical_and(z < last, k // 2 <= z))(lambda: up(slot).wait_send())
        pl.when(jnp.logical_and(z > 0, k // 2 >= z))(lambda: down(slot).wait_send())
        for g in range(2):
            r_over(g, k).wait_send()
            pl.when(k // 2 > z)(lambda: r_up(g, k).wait_send())
            pl.when(k // 2 < z)(lambda: r_down(g, k).wait_send())
    for g in range(2):
        r_side(g).wait_send()

    @pl.when(me < n - 1)
    def _():
        below_k.wait_send()
        below_v.wait_send()
        for p in range(HEADS // 2):
            to_below(p).wait_send()

    @pl.when(me > 0)
    def _():
        above_k.wait_send()
        above_v.wait_send()
        for p in range(HEADS // 2):
            to_above(p).wait_send()


def emit_kernel(*refs):
    sems = refs[-1]
    copies = [pltpu.make_async_copy(refs[i], refs[4 + i], sems.at[i]) for i in range(4)]
    for copy in copies:
        copy.start()
    for copy in copies:
        copy.wait()


VM = pl.BlockSpec(memory_space=pltpu.VMEM)
SM = pl.BlockSpec(memory_space=pltpu.SMEM)
ANY = pl.BlockSpec(memory_space=pl.ANY)
DMA = pltpu.SemaphoreType.DMA


def shape(dims, dtype):
    return jax.ShapeDtypeStruct(dims, dtype)


def per_device(n, queries, keys, values, out_grad, valid_counts, landmark_cols, landmark_rows):
    half = n // 2
    flat = (ROWS, WIDTH)
    block_rows = (PC, BLK, WIDTH)
    flat_t = (WIDTH, ROWS)
    pairs = (HEADS // 2, ROWS, 256)
    halves = (2, half, BLK, WIDTH)
    vmem = pltpu.VMEM
    results = pl.pallas_call(
        functools.partial(fused_kernel, n),
        out_shape=[shape(flat, BF16)] * 4,
        in_specs=[SM] * 3 + [VM] * 4,
        out_specs=[VM] * 4,
        scratch_shapes=[
            vmem((n, BLK, 2 * WIDTH), BF16),
            vmem(block_rows, BF16),
            vmem(block_rows, BF16),
            vmem(block_rows, BF16),
            vmem(block_rows, BF16),
            vmem((KEYS, WIDTH), BF16),
            vmem((KEYS, WIDTH), BF16),
            vmem((WIDTH, KEYS), BF16),
            vmem((WIDTH, KEYS), BF16),
            vmem(flat, BF16),
            vmem(flat, BF16),
            vmem(flat_t, BF16),
            vmem(flat_t, BF16),
            vmem(flat_t, F32),
            vmem(flat_t, F32),
            vmem((KEYS, ROWS), F32),
            vmem((HEADS, WIN, ROWS), F32),
            vmem((HEADS, 1, ROWS), F32),
            vmem((HEADS, 1, ROWS), F32),
            vmem((HEADS, WIN, ROWS), BF16),
            vmem((HEADS, WIN, ROWS), BF16),
            vmem(pairs, BF16),
            vmem(pairs, F32),
            vmem(pairs, BF16),
            vmem(pairs, BF16),
            vmem(pairs, BF16),
            vmem((2, NLAND + 1, BLK, WIDTH), BF16),
            vmem(halves, BF16),
            vmem(halves, BF16),
            vmem(halves, BF16),
            vmem(halves, BF16),
            vmem((2, BLK, WIDTH), BF16),
            vmem((2, BLK, WIDTH), F32),
            DMA((n,)),
            DMA((half,)),
            DMA((half,)),
            DMA((half,)),
            DMA((1,)),
            DMA((4,)),
            DMA((4,)),
            DMA((2, half)),
            DMA((2, half)),
            DMA((2, half)),
            DMA((2, half)),
            DMA((2, half)),
            DMA((2,)),
            DMA((2,)),
            DMA((2, HEADS // 2)),
            DMA((2, HEADS // 2)),
        ],
        compiler_params=pltpu.CompilerParams(
            collective_id=0, has_side_effects=True, vmem_limit_bytes=VMEM_LIMIT
        ),
    )(
        landmark_cols,
        landmark_rows,
        valid_counts,
        queries,
        keys.reshape(block_rows),
        values.reshape(block_rows),
        out_grad,
    )
    return tuple(
        pl.pallas_call(
            emit_kernel,
            out_shape=[shape(flat, BF16)] * 4,
            in_specs=[ANY] * 4,
            out_specs=[ANY] * 4,
            scratch_shapes=[DMA((4,))],
        )(*results)
    )


def solution(mesh):
    n = mesh.shape["prow"]
    tokens = P(("chars", "prow"), None)
    return jax.shard_map(
        functools.partial(per_device, n),
        mesh=mesh,
        in_specs=(tokens, tokens, tokens, tokens, P("chars", None), P("chars"), tokens),
        out_specs=(tokens, tokens, tokens, tokens),
        check_vma=False,
    )
```

time: 91.6 us -> 99.9 us (1.091)
  the two profiles are of different devices: /device:TPU:0 before, /device:TPU:1 now
where the time goes in v2:
time: 99.9 us; the launch traced here: 99.7 us
  Pallas kernels  97.7 us (98%)
  local copies, waits for them, and re-layouts  1.35 us (1%)
    pallas_call x1, Pallas kernels, per_device(): pl.pallas_call(functools.partial(fused_kernel, n), out_shape=[shape(flat,...  64.8 us
    pallas_call x1, Pallas kernels, per_device(): pl.pallas_call(emit_kernel, out_shape=[shape(flat, BF16)] * 4, in_specs=[...  32.9 us

profile of v2, /device:TPU:1, one launch (start us, length us, event | category | flops | bytes accessed | tf_op | source)
XLA Modules:
  0.0 99.7 jit_solution(8834057141462256921)
XLA Ops:
  0.6 0.0 copy-start
  0.6 0.7 copy-done
  1.3 0.7 copy.11.counts_ref
  2.0 64.8 %shard_map.102 = (bf16[256,512]{1,0:T(8,128)(2,1)}, bf16[256,512]{1,0:T(8,128)(2,1)}, bf16[256,512]{1,0:T(8,128)(2,1)}, bf16[256,512]{1,0:T(8,128)(2,1)}) custom-call(s32[16]{0:T(128)} %cols_ref.1, s32[1,4]{1,0:T(1,128)} %rows_ref.1, s32[16,4]{1,0:T(8,128)} %copy.11.counts_ref, bf16[256,512]{1,0:T(8,128)(2,1)} %q_ref.1, bf16[4,64,512]{2,1,0:T(8,128)(2,1)} %bitcast.2, ...), custom_call_target="tpu_custom_call" | custom-call | tf_op jit(solution)/shard_map/pallas_call | solution.py:557
  66.8 32.9 %shard_map.103 = (bf16[256,512]{1,0:T(8,128)(2,1)}, bf16[256,512]{1,0:T(8,128)(2,1)}, bf16[256,512]{1,0:T(8,128)(2,1)}, bf16[256,512]{1,0:T(8,128)(2,1)}) custom-call(bf16[256,512]{1,0:T(8,128)(2,1)} %get-tuple-element.8.refs_0_, bf16[256,512]{1,0:T(8,128)(2,1)} %get-tuple-element.9.refs_1_, bf16[256,512]{1,0:T(8,128)(2,1)} %get-tuple-element.10.refs_2_, ...), custom_call_target="tpu_custom_call" | custom-call | tf_op jit(solution)/shard_map/pallas_call | solution.py:626
Async XLA Ops:
  0.6 0.7 copy-start

commit v3 on v2

--- a/solution.py
+++ b/solution.py
@@ -528,17 +528,12 @@
 
 
 def emit_kernel(*refs):
-    sems = refs[-1]
-    copies = [pltpu.make_async_copy(refs[i], refs[4 + i], sems.at[i]) for i in range(4)]
-    for copy in copies:
-        copy.start()
-    for copy in copies:
-        copy.wait()
+    for source, result in zip(refs[:4], refs[4:]):
+        result[...] = source[...]
 
 
 VM = pl.BlockSpec(memory_space=pltpu.VMEM)
 SM = pl.BlockSpec(memory_space=pltpu.SMEM)
-ANY = pl.BlockSpec(memory_space=pl.ANY)
 DMA = pltpu.SemaphoreType.DMA
 
 
@@ -626,9 +621,8 @@
         pl.pallas_call(
             emit_kernel,
             out_shape=[shape(flat, BF16)] * 4,
-            in_specs=[ANY] * 4,
-            out_specs=[ANY] * 4,
-            scratch_shapes=[DMA((4,))],
+            in_specs=[VM] * 4,
+            out_specs=[VM] * 4,
         )(*results)
     )
 

time: 99.9 us -> 69.2 us (0.69)
  Pallas kernels: 97.7 us -> 67 us
    pallas_call x1, Pallas kernels: 32.9 us -> 2.17 us  [per_device(): pl.pallas_call(emit_kernel, out_shape=[shape(flat, BF16)] * 4, in_specs=[...]
where the time goes in v3:
time: 69.2 us; the launch traced here: 69 us
  Pallas kernels  67 us (97%)
  local copies, waits for them, and re-layouts  1.35 us (2%)
    pallas_call x1, Pallas kernels, per_device(): pl.pallas_call(functools.partial(fused_kernel, n), out_shape=[shape(flat,...  64.8 us
    pallas_call x1, Pallas kernels, per_device(): pl.pallas_call(emit_kernel, out_shape=[shape(flat, BF16)] * 4, in_specs=[...  2.17 us

profile of v3, /device:TPU:1, one launch (start us, length us, event | category | flops | bytes accessed | tf_op | source)
XLA Modules:
  0.0 69.0 jit_solution(1913912682325291540)
XLA Ops:
  0.6 0.0 copy-start
  0.6 0.7 copy-done
  1.3 0.7 copy.11.counts_ref
  2.0 64.8 %shard_map.102 = (bf16[256,512]{1,0:T(8,128)(2,1)}, bf16[256,512]{1,0:T(8,128)(2,1)}, bf16[256,512]{1,0:T(8,128)(2,1)}, bf16[256,512]{1,0:T(8,128)(2,1)}) custom-call(s32[16]{0:T(128)} %cols_ref.1, s32[1,4]{1,0:T(1,128)} %rows_ref.1, s32[16,4]{1,0:T(8,128)} %copy.11.counts_ref, bf16[256,512]{1,0:T(8,128)(2,1)} %q_ref.1, bf16[4,64,512]{2,1,0:T(8,128)(2,1)} %bitcast.2, ...), custom_call_target="tpu_custom_call" | custom-call | tf_op jit(solution)/shard_map/pallas_call | solution.py:552
  66.8 2.2 %shard_map.103 = (bf16[256,512]{1,0:T(8,128)(2,1)}, bf16[256,512]{1,0:T(8,128)(2,1)}, bf16[256,512]{1,0:T(8,128)(2,1)}, bf16[256,512]{1,0:T(8,128)(2,1)}) custom-call(bf16[256,512]{1,0:T(8,128)(2,1)} %get-tuple-element.8.refs_0_, bf16[256,512]{1,0:T(8,128)(2,1)} %get-tuple-element.9.refs_1_, bf16[256,512]{1,0:T(8,128)(2,1)} %get-tuple-element.10.refs_2_, ...), custom_call_target="tpu_custom_call" | custom-call | tf_op jit(solution)/shard_map/pallas_call | solution.py:621
Async XLA Ops:
  0.6 0.7 copy-start
